TPU v7x, 32 devices: a whole 2x2x4 slice. The times are simulated.
32 devices in a mesh: section: 2 (over core), expert: 16 (over z, y, x).
Axes of the slice: x: 2, y: 2, z: 4, core: 2. Of those that a mesh axis runs over, the one named last changes fastest.
Arguments:
- block_input: bfloat16 [2, 8192, 768], P(None, 'expert'), may hold values from -6 to 6
- cotangent: bfloat16 [2, 8192, 768], P(None, 'expert'), may hold values from -6 to 6
- expert_ids: int32 [2, 2, 8192, 2], P(None, None, 'expert'), may hold values from 0 to 15, all different within a row; in each aligned block of 512 rows (0 to 511, 512 to 1023, ..., all dimensions but the last counted through in order) at most 68 rows name the same one
- qkv_weight: bfloat16 [2, 768, 2304], P('section'), may hold values from -0.21875 to 0.21875
- query_bias: float32 [2, 768], P('section'), may hold values from -4 to 4
- value_bias: float32 [2, 768], P('section'), may hold values from -1.5 to 1.5
- proj_weight: bfloat16 [2, 768, 768], P('section'), may hold values from -1.75 to 1.75
- proj_bias: float32 [2, 768], P('section'), may hold values from -4 to 4
- attn_gain: float32 [2, 768], P('section'), may hold values from 0.25 to 1.75
- ffn_gain: float32 [2, 768], P('section'), may hold values from 0.25 to 1.75
- router_weight: bfloat16 [2, 768, 16], P('section'), may hold values from -0.4375 to 0.4375
- in_weight: bfloat16 [2, 16, 768, 3072], P('section', 'expert'), may hold values from -0.21875 to 0.21875
- out_weight: bfloat16 [2, 16, 3072, 768], P('section', 'expert'), may hold values from -0.109375 to 0.109375
Outputs:
- section_out: bfloat16 [2, 2, 8192, 768], P('section', None, 'expert')
- section_grad: float32 [2, 2, 8192, 768], P('section', None, 'expert')
- grad_qkv: float32 [2, 768, 2304], P('section')
- grad_qbias: float32 [2, 768], P('section')
- grad_vbias: float32 [2, 768], P('section')
- grad_proj: float32 [2, 768, 768], P('section')
- grad_pbias: float32 [2, 768], P('section')
- grad_attngain: float32 [2, 768], P('section')
- grad_ffngain: float32 [2, 768], P('section')
- grad_router: float32 [2, 768, 16], P('section')
- grad_win: bfloat16 [2, 16, 768, 3072], P('section', 'expert')
- grad_wout: bfloat16 [2, 16, 3072, 768], P('section', 'expert')
Inputs may be any that keep to these rules, and one draw needn't show every extreme that they name: `expert_ids`: A token's 2 ids differ. For each layer and micro-batch, among the choices of the 512 tokens of one device, no expert is named more than 68 times, a bound that some block reaches.
All inputs are finite; a program needn't handle non-finite values.
Results may differ from a plain program's by a relative error of at most 0.02.
Values may be sent and summed in bfloat16 or wider, within the bound.
A program may use at most 384 MiB of HBM per device.

v0:
```python
import jax
import jax.numpy as jnp
from jax import lax
from jax.sharding import PartitionSpec as P

HD = 64
EPS = 1e-06
NEG = -1e30
BF = jnp.bfloat16
F32 = jnp.float32
HIGH = lax.Precision.HIGHEST
SWAP = [(0, 1), (1, 0)]


def dot(a, b, dims, kind=F32, precision=None):
    return lax.dot_general(
        a, b, (dims, ((), ())), precision=precision, preferred_element_type=F32
    ).astype(kind)


NN = ((1,), (0,))
NT = ((1,), (1,))
TN = ((0,), (0,))


def capacity_of(tokens, choices, experts):
    return tokens * choices // experts + max(1, tokens * choices // (16 * experts))


def inverse_rms(field):
    return lax.rsqrt(jnp.mean(field * field, axis=-1, keepdims=True) + EPS)


def norm_back(field, gain, grad):
    scale = inverse_rms(field)
    unit = field * scale
    grad_gain = jnp.sum(grad * unit, axis=0)
    scaled = grad * gain
    grad_field = scale * (scaled - unit * jnp.mean(scaled * unit, axis=-1, keepdims=True))
    return (grad_field, grad_gain)


def causal_scores(queries, key_rows):
    scores = jnp.einsum("qhd,khd->hqk", queries, key_rows, preferred_element_type=F32) * HD ** (
        -0.5
    )
    length = scores.shape[-1]
    causal = jnp.arange(length)[:, None] >= jnp.arange(length)[None, :]
    return jnp.where(causal[None], scores, NEG)


def attend_forward(queries, key_rows, value_rows):
    tokens, width = queries.shape
    shape = (tokens, width // HD, HD)
    scores = causal_scores(queries.reshape(shape), key_rows.reshape(shape))
    row_max = jnp.max(scores, axis=-1, keepdims=True)
    weights = jnp.exp(scores - row_max)
    row_total = jnp.sum(weights, axis=-1, keepdims=True)
    prob_low = (weights / row_total).astype(BF)
    attended = jnp.einsum(
        "hqk,khd->qhd", prob_low, value_rows.reshape(shape), preferred_element_type=F32
    )
    return (
        attended.astype(BF).reshape(tokens, width),
        row_max[..., 0] + jnp.log(row_total[..., 0]),
    )


def attend_backward(queries, key_rows, value_rows, log_total, grad_out):
    tokens, width = queries.shape
    shape = (tokens, width // HD, HD)
    queries, key_rows, value_rows, grad_out = (
        part.reshape(shape) for part in (queries, key_rows, value_rows, grad_out)
    )
    scores = causal_scores(queries, key_rows)
    weights = jnp.exp(scores - log_total[..., None])
    grad_probs = jnp.einsum("qhd,khd->hqk", grad_out, value_rows, preferred_element_type=F32)
    inner = jnp.sum(weights * grad_probs, axis=-1, keepdims=True)
    grad_scores = (weights * (grad_probs - inner)).astype(BF)
    grad_value = jnp.einsum(
        "hqk,qhd->khd", weights.astype(BF), grad_out, preferred_element_type=F32
    )
    grad_query = jnp.einsum(
        "hqk,khd->qhd", grad_scores, key_rows, preferred_element_type=F32
    ) * HD ** (-0.5)
    grad_key = jnp.einsum(
        "hqk,qhd->khd", grad_scores, queries, preferred_element_type=F32
    ) * HD ** (-0.5)
    return tuple(
        (part.astype(BF).reshape(tokens, width) for part in (grad_query, grad_key, grad_value))
    )


def gelu_and_slope(hidden):
    root = 0.7978845608028654
    square = hidden * hidden
    bent = jnp.tanh(root * hidden * (1.0 + 0.044715 * square))
    half = 0.5 * (1.0 + bent)
    slope = half + 0.5 * hidden * (1.0 - bent * bent) * root * (1.0 + 0.134145 * square)
    return (hidden * half, slope)


def route_plan(route_ids, experts, capacity):
    tokens = route_ids.shape[0]
    lanes = jnp.arange(experts, dtype=jnp.int32)[None, :]
    first = (route_ids[:, 0:1] == lanes).astype(F32)
    second = (route_ids[:, 1:2] == lanes).astype(F32)
    places = jnp.arange(tokens, dtype=jnp.int32)
    earlier = (places[:, None] > places[None, :]).astype(BF)
    counts = dot(earlier, (first + second).astype(BF), NN)
    ranks = [jnp.sum(counts * hot, axis=-1).astype(jnp.int32) for hot in (first, second)]
    slots = [route_ids[:, j] * capacity + ranks[j] for j in range(2)]
    row = jnp.arange(experts * capacity, dtype=jnp.int32)[:, None]
    place = [(row == slot[None, :]).astype(BF) for slot in slots]
    return (first, second, place[0], place[1])


def exchange(rows, experts):
    total, width = rows.shape
    moved = lax.all_to_all(
        rows.reshape(experts, total // experts, width),
        "expert",
        split_axis=0,
        concat_axis=0,
        tiled=True,
    )
    return moved.reshape(total, width)


def layer_forward(current, plan, weights):
    qkv, qbias, vbias, proj, pbias, gain_attn, gain_ffn, router, win, wout = weights
    first, second, place0, place1 = plan
    width = current.shape[1]
    experts = router.shape[1]
    normed = (current * inverse_rms(current) * gain_attn).astype(BF)
    packed = dot(normed, qkv, NN)
    queries = (packed[:, :width] + qbias).astype(BF)
    key_rows = packed[:, width : 2 * width].astype(BF)
    value_rows = (packed[:, 2 * width :] + vbias).astype(BF)
    attended, log_total = attend_forward(queries, key_rows, value_rows)
    middle = current + (dot(attended, proj, NN) + pbias)
    routed = (middle * inverse_rms(middle) * gain_ffn).astype(BF)
    logits = dot(routed, router, NN)
    gap = jnp.sum(logits * (first - second), axis=-1, keepdims=True)
    gate0, gate1 = (jax.nn.sigmoid(gap), jax.nn.sigmoid(-gap))
    arrived = exchange(dot(place0 + place1, routed, NN, BF), experts)
    hidden = dot(arrived, win, NN)
    active, slope = gelu_and_slope(hidden)
    active, slope = (active.astype(BF), slope.astype(BF))
    produced = dot(active, wout, NN, BF)
    returned = exchange(produced, experts)
    combined0 = dot(place0, returned, TN, BF)
    combined1 = dot(place1, returned, TN, BF)
    outputs = middle + (gate0 * combined0.astype(F32) + gate1 * combined1.astype(F32))
    kept = (
        current,
        normed,
        queries,
        key_rows,
        value_rows,
        log_total,
        attended,
        middle,
        routed,
        gate0,
        gate1,
        combined0,
        combined1,
        arrived,
        active,
        slope,
    )
    return (outputs, kept)


def layer_backward(seed, kept, plan, weights):
    qkv, qbias, vbias, proj, pbias, gain_attn, gain_ffn, router, win, wout = weights
    first, second, place0, place1 = plan
    (
        current,
        normed,
        queries,
        key_rows,
        value_rows,
        log_total,
        attended,
        middle,
        routed,
        gate0,
        gate1,
        combined0,
        combined1,
        arrived,
        active,
        slope,
    ) = kept
    experts = router.shape[1]
    outgoing = dot(place0, (gate0 * seed).astype(BF), NN) + dot(
        place1, (gate1 * seed).astype(BF), NN
    )
    arriving = exchange(outgoing.astype(BF), experts)
    grad_active = dot(arriving, wout, NT)
    grad_hidden = (grad_active * slope.astype(F32)).astype(BF)
    returning = exchange(dot(grad_hidden, win, NT, BF), experts)
    grad_wout = dot(active, arriving, TN, BF)
    grad_win = dot(arrived, grad_hidden, TN, BF)
    grad_gap = (
        gate0
        * gate1
        * jnp.sum(seed * (combined0.astype(F32) - combined1.astype(F32)), axis=-1, keepdims=True)
    )
    grad_logits = grad_gap * (first - second)
    grad_router = dot(grad_logits, routed.astype(F32), TN, precision=HIGH)
    grad_routed = dot(place0 + place1, returning, TN) + dot(
        grad_logits, router.astype(F32), NT, precision=HIGH
    )
    grad_middle, grad_gain_ffn = norm_back(middle, gain_ffn, grad_routed)
    grad_middle = grad_middle + seed
    grad_branch = grad_middle.astype(BF)
    grad_pbias = jnp.sum(grad_branch.astype(F32), axis=0)
    grad_proj = dot(attended, grad_branch, TN, BF)
    grad_attended = dot(grad_branch, proj, NT, BF)
    grad_query, grad_key, grad_value = attend_backward(
        queries, key_rows, value_rows, log_total, grad_attended
    )
    grad_packed = jnp.concatenate([grad_query, grad_key, grad_value], axis=1)
    grad_qbias = jnp.sum(grad_query.astype(F32), axis=0)
    grad_vbias = jnp.sum(grad_value.astype(F32), axis=0)
    grad_qkv = [dot(normed, part, TN, BF) for part in (grad_query, grad_key, grad_value)]
    grad_normed = dot(grad_packed, qkv, NT)
    grad_current, grad_gain_attn = norm_back(current, gain_attn, grad_normed)
    grad_current = grad_current + grad_middle
    small = jnp.concatenate(
        [
            jnp.stack([grad_qbias, grad_vbias, grad_pbias, grad_gain_attn, grad_gain_ffn]),
            grad_router,
        ]
    )
    small = jnp.pad(small, ((0, -small.shape[0] % 32), (0, 0)))
    shared = jnp.concatenate(grad_qkv + [grad_proj, small.astype(BF)])
    return (grad_current, shared, grad_win, grad_wout)


def reduce_shared(shared, section):
    half = shared.shape[0] // 2
    own = lax.dynamic_slice_in_dim(shared, section * half, half, 0)
    other = lax.dynamic_slice_in_dim(shared, (1 - section) * half, half, 0)
    other = lax.ppermute(other, "section", SWAP)
    return lax.psum((own.astype(F32) + other.astype(F32)).astype(BF), "expert")


def both(own, other, is_first):
    return (jnp.where(is_first, own, other), jnp.where(is_first, other, own))


def shards(
    block_input,
    cotangent,
    expert_ids,
    qkv_weight,
    query_bias,
    value_bias,
    proj_weight,
    proj_bias,
    attn_gain,
    ffn_gain,
    router_weight,
    in_weight,
    out_weight,
):
    section = lax.axis_index("section")
    is_first = section == 0
    width = block_input.shape[2]
    experts = router_weight.shape[2]
    tokens = block_input.shape[1]
    capacity = capacity_of(tokens, expert_ids.shape[3], experts)

    def gathered(array):
        return lax.all_gather(array, "section", axis=0, tiled=True)

    vectors = gathered(jnp.stack([query_bias, value_bias, proj_bias, attn_gain, ffn_gain], axis=1))
    qkv_all, proj_all, router_all = (
        gathered(part) for part in (qkv_weight, proj_weight, router_weight)
    )
    win_all, wout_all = (gathered(in_weight), gathered(out_weight))
    layers = [
        (
            qkv_all[l],
            vectors[l, 0],
            vectors[l, 1],
            proj_all[l],
            vectors[l, 2],
            vectors[l, 3],
            vectors[l, 4],
            router_all[l],
            win_all[l, 0],
            wout_all[l, 0],
        )
        for l in range(2)
    ]
    rows = lax.dynamic_index_in_dim(block_input, section, 0, keepdims=False)
    seed = lax.dynamic_index_in_dim(cotangent, section, 0, keepdims=False)
    ids = lax.dynamic_index_in_dim(expert_ids, section, 1, keepdims=False)
    plans = [route_plan(ids[l], experts, capacity) for l in range(2)]
    out0, kept0 = layer_forward(rows.astype(F32), plans[0], layers[0])
    out0 = out0.astype(BF)
    out1, kept1 = layer_forward(out0.astype(F32), plans[1], layers[1])
    out1 = out1.astype(BF)
    out_other = lax.ppermute(jnp.where(is_first, out1, out0), "section", SWAP)
    section_out = jnp.stack(both(jnp.where(is_first, out0, out1), out_other, is_first))
    grad1, shared1, win1, wout1 = layer_backward(seed.astype(F32), kept1, plans[1], layers[1])
    grad1 = grad1.astype(BF)
    up, down = ([(0, 1)], [(1, 0)])
    win1_other = lax.ppermute(win1, "section", up)
    wout1_other = lax.ppermute(wout1, "section", up)
    grad1_other = lax.ppermute(grad1, "section", up)
    total1 = reduce_shared(shared1, section)
    total1_other = lax.ppermute(total1, "section", up)
    grad0, shared0, win0, wout0 = layer_backward(grad1.astype(F32), kept0, plans[0], layers[0])
    win0_other = lax.ppermute(win0, "section", down)
    wout0_other = lax.ppermute(wout0, "section", down)
    grad0_other = lax.ppermute(grad0, "section", down)
    shared0, total1 = lax.optimization_barrier((shared0, total1))
    total0 = reduce_shared(shared0, section)
    total0_other = lax.ppermute(total0, "section", down)
    section_grad = jnp.stack(
        [
            jnp.where(is_first, grad0, grad1_other.astype(F32)),
            jnp.where(is_first, grad0_other, grad1.astype(F32)),
        ]
    )

    def summed(first, first_other, second, second_other):
        return jnp.where(
            is_first,
            first.astype(F32) + first_other.astype(F32),
            second.astype(F32) + second_other.astype(F32),
        ).astype(BF)

    grad_win = summed(win0, win0_other, win1, win1_other)
    grad_wout = summed(wout0, wout0_other, wout1, wout1_other)
    total = jnp.concatenate(
        [jnp.where(is_first, total0, total1_other), jnp.where(is_first, total0_other, total1)]
    ).astype(F32)
    grad_qkv = jnp.concatenate([total[i * width : (i + 1) * width] for i in range(3)], axis=1)
    grad_proj = total[3 * width : 4 * width]
    small = total[4 * width : 4 * width + 5 + experts]
    return (
        section_out[None],
        section_grad[None],
        grad_qkv[None],
        small[0][None],
        small[1][None],
        grad_proj[None],
        small[2][None],
        small[3][None],
        small[4][None],
        small[5:].T[None],
        grad_win[None, None],
        grad_wout[None, None],
    )


def solution(mesh):
    vector, matrix = (P("section", None), P("section", None, None))
    expert = P("section", "expert", None, None)
    rows = P("section", None, "expert", None)
    return jax.shard_map(
        shards,
        mesh=mesh,
        in_specs=(
            P(None, "expert", None),
            P(None, "expert", None),
            P(None, None, "expert", None),
            matrix,
            vector,
            vector,
            matrix,
            vector,
            vector,
            vector,
            matrix,
            expert,
            expert,
        ),
        out_specs=(
            rows,
            rows,
            matrix,
            vector,
            vector,
            matrix,
            vector,
            vector,
            vector,
            matrix,
            expert,
            expert,
        ),
        check_vma=False,
    )
```

profile of v0, /device:TPU:1, one launch (start us, length us, event | category | flops | bytes accessed | tf_op | source)
XLA Modules:
  0.0 987.2 jit_solution(1497431920451466052)
XLA Ops:
  14.0 15.9 %all-gather.5.cloned.1.call-done = bf16[2,768,2304]{2,1,0:T(8,128)(2,1)} async-done(((bf16[1,768,2304]{2,1,0:T(8,128)(2,1)}), bf16[2,768,2304]{2,1,0:T(8,128)(2,1)}) %all-gather.5.cloned.1.call-update) | async-done | bytes 7077904 | tf_op jit(solution)/shard_map/all_gather | solution.py:279
  30.0 4.1 fusion.31
  42.8 3.6 fusion.116
  55.3 58.5 %all_to_all.40 = bf16[16,68,768]{2,1,0:T(8,128)(2,1)} all-to-all(bf16[16,68,768]{2,1,0:T(8,128)(2,1)} %reshape.378), channel_id=1, replica_groups=mesh['section'=2,'expert'=16] {'expert'}, dimensions={0} | all-to-all | bytes 3342336 | tf_op jit(solution)/shard_map/all_to_all | solution.py:120
  117.2 11.0 %fusion.19 = f32[1088,3072]{1,0:T(8,128)} fusion(bf16[1088,768]{1,0:T(8,128)(2,1)} %reshape.379, bf16[2,1,768,3072]{3,2,1,0:T(8,128)(2,1)} %all-gather.9.cloned.1.call-done), kind=kOutput, calls=%fused_computation.53 | convolution fusion | flops 5133828096 | bytes 19759104 | tf_op jit(solution)/shard_map/dot_general | solution.py:16
  128.2 13.0 %fusion.26 = bf16[1088,768]{1,0:T(8,128)(2,1)} fusion(bf16[2,1,3072,768]{3,2,1,0:T(8,128)(2,1)} %all-gather.11.cloned.1.call-done, f32[1088,3072]{1,0:T(8,128)} %fusion.19), kind=kOutput, calls=%fused_computation.64 | convolution fusion | flops 5164744704 | bytes 19759104 | tf_op jit(solution)/shard_map/dot_general | solution.py:16
  144.6 4.6 all-to-all-start.1
  154.8 30.5 %all-to-all-done.1 = bf16[16,68,768]{2,1,0:T(8,128)(2,1)} async-done(((bf16[16,68,768]{2,1,0:T(8,128)(2,1)}), bf16[16,68,768]{2,1,0:T(8,128)(2,1)}, u32[]{:S(2)}, u32[]{:S(2)}) %all-to-all-start.1) | async-done | bytes 1671200 | tf_op jit(solution)/shard_map/all_to_all | solution.py:120
  192.3 4.4 fusion.33
  204.7 4.0 fusion.115
  215.8 50.3 %all_to_all.41 = bf16[16,68,768]{2,1,0:T(8,128)(2,1)} all-to-all(bf16[16,68,768]{2,1,0:T(8,128)(2,1)} %reshape.386), channel_id=1, replica_groups=mesh['section'=2,'expert'=16] {'expert'}, dimensions={0} | all-to-all | bytes 3342336 | tf_op jit(solution)/shard_map/all_to_all | solution.py:120
  269.5 7.7 fusion.22
  277.2 4.9 copy-done.130
  282.1 11.3 %fusion.24 = bf16[1088,768]{1,0:T(8,128)(2,1)} fusion(bf16[2,1,3072,768]{3,2,1,0:T(8,128)(2,1)} %all-gather.11.cloned.1.call-done, f32[1088,3072]{1,0:T(8,128)S(1)} %fusion.22), kind=kOutput, calls=%fused_computation.62 | convolution fusion | flops 5164744704 | bytes 19759104 | tf_op jit(solution)/shard_map/dot_general | solution.py:16
  296.7 4.7 all-to-all-start.3
  301.8 35.8 %all-to-all-done.3 = bf16[16,68,768]{2,1,0:T(8,128)(2,1)} async-done(((bf16[16,68,768]{2,1,0:T(8,128)(2,1)}), bf16[16,68,768]{2,1,0:T(8,128)(2,1)}, u32[]{:S(2)}, u32[]{:S(2)}) %all-to-all-start.3) | async-done | bytes 1671200 | tf_op jit(solution)/shard_map/all_to_all | solution.py:120
  353.4 50.5 %all_to_all.42 = bf16[16,68,768]{2,1,0:T(8,128)(2,1)} all-to-all(bf16[16,68,768]{2,1,0:T(8,128)(2,1)} %reshape.390), channel_id=1, replica_groups=mesh['section'=2,'expert'=16] {'expert'}, dimensions={0} | all-to-all | bytes 3342336 | tf_op jit(solution)/shard_map/all_to_all | solution.py:120
  407.3 15.2 %fusion = bf16[1088,3072]{1,0:T(8,128)(2,1)S(1)} fusion(bf16[1088,768]{1,0:T(8,128)(2,1)} %reshape.391, f32[1088,3072]{1,0:T(8,128)} %copy-done.130, bf16[2,1,3072,768]{3,2,1,0:T(8,128)(2,1)} %all-gather.11.cloned.1.call-done), kind=kOutput, calls=%fused_computation.22 | convolution fusion | flops 5200674816 | bytes 26443776 | tf_op jit(solution)/shard_map/dot_general | solution.py:16
  425.3 8.9 fusion.25
  437.7 4.8 all-to-all-start.5
  443.6 34.9 %all-to-all-done.5 = bf16[16,68,768]{2,1,0:T(8,128)(2,1)} async-done(((bf16[16,68,768]{2,1,0:T(8,128)(2,1)}), bf16[16,68,768]{2,1,0:T(8,128)(2,1)}, u32[]{:S(2)}, u32[]{:S(2)}) %all-to-all-start.5) | async-done | bytes 1671200 | tf_op jit(solution)/shard_map/all_to_all | solution.py:120
  490.9 8.1 bitcast_reduce_fusion.2
  499.0 9.5 multiply_reduce_fusion.1
  508.5 7.5 multiply_convert_fusion.3
  527.9 3.6 fusion.29
  534.9 9.2 all-to-all-start.6
  544.1 13.1 %convolution_convert_fusion = bf16[3072,768]{1,0:T(8,128)(2,1)} fusion(bf16[1088,768]{1,0:T(8,128)(2,1)} %reshape.391, f32[1088,3072]{1,0:T(8,128)} %copy-done.130), kind=kOutput, calls=%fused_computation.37 | convolution fusion | flops 5166268416 | bytes 19759104 | tf_op jit(solution)/shard_map/dot_general | solution.py:16
  570.8 9.5 all-to-all-done.6
  582.6 15.3 %fusion.1 = bf16[1088,3072]{1,0:T(8,128)(2,1)S(1)} fusion(bf16[1088,768]{1,0:T(8,128)(2,1)S(1)} %reshape.399, f32[1088,3072]{1,0:T(8,128)} %fusion.19, bf16[2,1,3072,768]{3,2,1,0:T(8,128)(2,1)} %all-gather.11.cloned.1.call-done), kind=kOutput, calls=%fused_computation.23 | convolution fusion | flops 5200674816 | bytes 26443776 | tf_op jit(solution)/shard_map/dot_general | solution.py:16
  600.8 8.9 fusion.27
  613.1 8.8 all-to-all-start.7
  621.9 10.5 %convolution_convert_fusion.2 = bf16[768,3072]{1,0:T(8,128)(2,1)} fusion(bf16[1088,768]{1,0:T(8,128)(2,1)} %reshape.387, bf16[1088,3072]{1,0:T(8,128)(2,1)} %copy-done.128), kind=kOutput, calls=%fused_computation.39 | convolution fusion | flops 5136187392 | bytes 13074432 | tf_op jit(solution)/shard_map/dot_general | solution.py:16
  636.8 4.4 add_convert_fusion.3
  641.2 10.8 %convolution_convert_fusion.3 = bf16[768,3072]{1,0:T(8,128)(2,1)} fusion(bf16[1088,768]{1,0:T(8,128)(2,1)} %reshape.379, bf16[1088,3072]{1,0:T(8,128)(2,1)} %copy-done.129), kind=kOutput, calls=%fused_computation.40 | convolution fusion | flops 5136187392 | bytes 13074432 | tf_op jit(solution)/shard_map/dot_general | solution.py:16
  652.1 11.3 %collective-permute-start.7 = (bf16[768,3072]{1,0:T(8,128)(2,1)}, bf16[768,3072]{1,0:T(8,128)(2,1)}, u32[]{:S(2)}, u32[]{:S(2)}) collective-permute-start(bf16[768,3072]{1,0:T(8,128)(2,1)} %convolution_convert_fusion.3), channel_id=1, source_target_pairs={{16,0},{17,1},{18,2},{19,3},{20,4},{21,5},{22,6},{23,7},{24,8},{25... | collective-permute-start | bytes 14155784 | tf_op jit(solution)/shard_map/ppermute | solution.py:320
  672.0 7.6 bitcast_reduce_fusion
  679.6 9.8 multiply_reduce_fusion
  689.4 7.2 multiply_convert_fusion.2
  699.6 5.0 multiply_convert_fusion.4
  704.6 5.7 fusion.74
  720.2 67.2 %all-reduce.5.cloned.1.call-done = bf16[1552,768]{1,0:T(8,128)(2,1)} async-done(((bf16[1552,768]{1,0:T(8,128)(2,1)}), bf16[1552,768]{1,0:T(8,128)(2,1)}) %all-reduce.5.cloned.1.call-update) | async-done | bytes 2383888 | tf_op jit(solution)/shard_map/psum | solution.py:249
  789.8 12.8 %convolution_convert_fusion.1 = bf16[3072,768]{1,0:T(8,128)(2,1)} fusion(bf16[1088,768]{1,0:T(8,128)(2,1)S(1)} %copy-done.28, f32[1088,3072]{1,0:T(8,128)} %fusion.19), kind=kOutput, calls=%fused_computation.38 | convolution fusion | flops 5166268416 | bytes 19759104 | tf_op jit(solution)/shard_map/dot_general | solution.py:16
  802.6 4.1 collective-permute-start.9
  806.7 3.9 add_convert_fusion.2
  824.7 117.9 %all-reduce.7.cloned.1.call-done = bf16[1552,768]{1,0:T(8,128)(2,1)} async-done(((bf16[1552,768]{1,0:T(8,128)(2,1)}), bf16[1552,768]{1,0:T(8,128)(2,1)}) %all-reduce.7.cloned.1.call-update) | async-done | bytes 2383888 | tf_op jit(solution)/shard_map/psum | solution.py:249
  942.6 4.1 collective-permute-start.6
  946.7 12.9 %fusion.14 = bf16[1,1,768,3072]{3,2,1,0:T(8,128)(2,1)} fusion(bf16[768,3072]{1,0:T(8,128)(2,1)} %collective-permute-done.8, bf16[768,3072]{1,0:T(8,128)(2,1)} %convolution_convert_fusion.2, bf16[768,3072]{1,0:T(8,128)(2,1)} %collective-permute-done.7, bf16[768,3072]{1,0:T(8,128)(2,1)} %convolution_convert_fusion.3, pred[]{:T(512)S(6)} %eq.115), kind=kLoop, calls=%fused_computation.44 | loop fusion | flops 18874368 | bytes 23592960 | tf_op jit(solution)/shard_map/broadcast_in_dim | solution.py:359
  959.6 10.9 %fusion.15 = bf16[1,1,3072,768]{3,2,1,0:T(8,128)(2,1)} fusion(bf16[3072,768]{1,0:T(8,128)(2,1)} %collective-permute-done.10, bf16[3072,768]{1,0:T(8,128)(2,1)} %convolution_convert_fusion, bf16[3072,768]{1,0:T(8,128)(2,1)} %collective-permute-done.9, bf16[3072,768]{1,0:T(8,128)(2,1)} %convolution_convert_fusion.1, pred[]{:T(512)S(6)} %eq.115), kind=kLoop, calls=%fused_computation.45 | loop fusion | flops 18874368 | bytes 23592960 | tf_op jit(solution)/shard_map/broadcast_in_dim | solution.py:360
  (440 shorter events, 192.7 us)
Async XLA Ops:
  7.2 22.8 %all-gather.5.cloned.1.call-start = ((), (), s32[]{:S(2)}) async-start(), calls=%async_computation.8 | async-start | bytes 10616832 | tf_op jit(solution)/shard_map/all_gather | solution.py:279
  7.9 38.5 %all-gather.7.cloned.1.call-start = ((), (), s32[]{:S(2)}) async-start(), calls=%async_computation.9 | async-start | bytes 3538944 | tf_op jit(solution)/shard_map/all_gather | solution.py:279
  8.7 108.6 %all-gather.9.cloned.1.call-start = ((), (), s32[]{:S(2)}) async-start(), calls=%async_computation.10 | async-start | bytes 14155776 | tf_op jit(solution)/shard_map/all_gather | solution.py:279
  9.5 118.7 %all-gather.11.cloned.1.call-start = ((), (), s32[]{:S(2)}) async-start(), calls=%async_computation.11 | async-start | bytes 14155776 | tf_op jit(solution)/shard_map/all_gather | solution.py:279
  11.1 18.9 %copy-start.93 = (f32[512]{0:T(512)}, f32[512]{0:T(512)S(1)}, u32[]{:S(2)}) copy-start(f32[512]{0:T(512)S(1)} %add_rsqrt_fusion.3) | copy-start | bytes 6148
  11.1 141.6 %copy-start.65 = (s32[512,1]{0,1:T(1,128)}, s32[512,1]{0,1:T(1,128)S(1)}, u32[]{:S(2)}) copy-start(s32[512,1]{0,1:T(1,128)S(1)} %get-tuple-element.69) | copy-start | bytes 6148
  11.1 142.2 %copy-start.69 = (s32[512,1]{0,1:T(1,128)}, s32[512,1]{0,1:T(1,128)S(1)}, u32[]{:S(2)}) copy-start(s32[512,1]{0,1:T(1,128)S(1)} %get-tuple-element.70) | copy-start | bytes 6148
  11.1 142.8 %copy-start.61 = (s32[512,1]{0,1:T(1,128)}, s32[512,1]{0,1:T(1,128)S(1)}, u32[]{:S(2)}) copy-start(s32[512,1]{0,1:T(1,128)S(1)} %get-tuple-element.105) | copy-start | bytes 6148
  11.1 142.8 %copy-start.63 = (s32[512,1]{0,1:T(1,128)}, s32[512,1]{0,1:T(1,128)S(1)}, u32[]{:S(2)}) copy-start(s32[512,1]{0,1:T(1,128)S(1)} %get-tuple-element.106) | copy-start | bytes 6148
  11.4 38.0 %copy-start.108 = (s32[512]{0:T(512)}, s32[512]{0:T(512)S(1)}, u32[]{:S(2)}) copy-start(s32[512]{0:T(512)S(1)} %convert_add_fusion.8) | copy-start | bytes 6148
  11.4 37.9 %copy-start.111 = (s32[512]{0:T(512)}, s32[512]{0:T(512)S(1)}, u32[]{:S(2)}) copy-start(s32[512]{0:T(512)S(1)} %convert_add_fusion.7) | copy-start | bytes 6148
  14.0 15.9 %copy-start.82 = (f32[768]{0:T(1024)}, f32[768]{0:T(1024)S(1)}, u32[]{:S(2)}) copy-start(f32[768]{0:T(1024)S(1)} %get-tuple-element.33) | copy-start | bytes 9220
  14.0 35.1 %copy-start.57 = (f32[768]{0:T(1024)}, f32[768]{0:T(1024)S(1)}, u32[]{:S(2)}) copy-start(f32[768]{0:T(1024)S(1)} %get-tuple-element.29) | copy-start | bytes 9220
  49.1 140.6 %copy-start.3 = (f32[512,768]{1,0:T(8,128)}, f32[512,768]{1,0:T(8,128)S(1)}, u32[]{:S(2)}) copy-start(f32[512,768]{1,0:T(8,128)S(1)} %get-tuple-element.81) | copy-start | bytes 4718596
  49.4 104.5 %copy-start.13 = (bf16[512,768]{1,0:T(8,128)(2,1)}, bf16[512,768]{1,0:T(8,128)(2,1)S(1)}, u32[]{:S(2)}) copy-start(bf16[512,768]{1,0:T(8,128)(2,1)S(1)} %multiply_convert_fusion.9) | copy-start | bytes 2359300
  144.6 40.7 %all-to-all-start.1 = ((bf16[16,68,768]{2,1,0:T(8,128)(2,1)}), bf16[16,68,768]{2,1,0:T(8,128)(2,1)}, u32[]{:S(2)}, u32[]{:S(2)}) async-start(bf16[16,68,768]{2,1,0:T(8,128)(2,1)} %reshape.380), calls=%async_computation.1 | async-start | bytes 3538944 | tf_op jit(solution)/shard_map/all_to_all | solution.py:120
  296.7 40.8 %all-to-all-start.3 = ((bf16[16,68,768]{2,1,0:T(8,128)(2,1)}), bf16[16,68,768]{2,1,0:T(8,128)(2,1)}, u32[]{:S(2)}, u32[]{:S(2)}) async-start(bf16[16,68,768]{2,1,0:T(8,128)(2,1)} %reshape.388), calls=%async_computation.3 | async-start | bytes 3538944 | tf_op jit(solution)/shard_map/all_to_all | solution.py:120
  346.3 96.3 %copy-start.78 = (f32[512]{0:T(512)}, f32[512]{0:T(512)S(1)}, u32[]{:S(2)}) copy-start(f32[512]{0:T(512)S(1)} %get-tuple-element.73) | copy-start | bytes 6148
  437.7 40.9 %all-to-all-start.5 = ((bf16[16,68,768]{2,1,0:T(8,128)(2,1)}), bf16[16,68,768]{2,1,0:T(8,128)(2,1)}, u32[]{:S(2)}, u32[]{:S(2)}) async-start(bf16[16,68,768]{2,1,0:T(8,128)(2,1)} %reshape.392), calls=%async_computation.5 | async-start | bytes 3538944 | tf_op jit(solution)/shard_map/all_to_all | solution.py:120
  490.9 17.6 %slice-start.3 = ((s8[12582912]{0:T(1024)(128)(4,1)}), s8[4194304]{0:T(1024)(128)(4,1)S(1)}, s32[]{:S(2)}) async-start(s8[12582912]{0:T(1024)(128)(4,1)} %bitcast.235), calls=%async_computation.17 | async-start | bytes 8388608
  490.9 17.6 %slice-start.4 = ((s8[12582912]{0:T(1024)(128)(4,1)}), s8[4194304]{0:T(1024)(128)(4,1)S(1)}, s32[]{:S(2)}) async-start(s8[12582912]{0:T(1024)(128)(4,1)} %bitcast.235), calls=%async_computation.18 | async-start | bytes 8388608
  534.9 45.4 %all-to-all-start.6 = ((bf16[16,68,768]{2,1,0:T(8,128)(2,1)}), bf16[16,68,768]{2,1,0:T(8,128)(2,1)}, u32[]{:S(2)}, u32[]{:S(2)}) async-start(bf16[16,68,768]{2,1,0:T(8,128)(2,1)} %reshape.398), calls=%async_computation.6 | async-start | bytes 3538944 | tf_op jit(solution)/shard_map/all_to_all | solution.py:120
  544.1 13.7 %copy-start.99 = (bf16[768]{0:T(1024)(128)(2,1)S(1)}, bf16[768]{0:T(1024)(128)(2,1)}, u32[]{:S(2)}) copy-start(bf16[768]{0:T(1024)(128)(2,1)} %get-tuple-element.38) | copy-start | bytes 4612
  544.1 14.3 %copy-start.101 = (bf16[12,64]{1,0:T(8,128)(2,1)S(1)}, bf16[12,64]{1,0:T(8,128)(2,1)}, u32[]{:S(2)}) copy-start(bf16[12,64]{1,0:T(8,128)(2,1)} %get-tuple-element.103) | copy-start | bytes 4612
  544.1 16.2 %copy-start.56 = (bf16[16,768]{1,0:T(8,128)(2,1)S(1)}, bf16[16,768]{1,0:T(8,128)(2,1)}, u32[]{:S(2)}) copy-start(bf16[16,768]{1,0:T(8,128)(2,1)} %convolution_convert_fusion.16) | copy-start | bytes 73732
  569.0 67.8 %collective-permute-start.3 = (bf16[1552,768]{1,0:T(8,128)(2,1)}, bf16[1552,768]{1,0:T(8,128)(2,1)}, u32[]{:S(2)}, u32[]{:S(2)}) collective-permute-start(bf16[1552,768]{1,0:T(8,128)(2,1)} %constant_dynamic-slice_fusion.1), channel_id=1, source_target_pairs={{0,16},{16,0},{1,17},{17,1},{2,18},{18,2},{3,19},{19,3},{4,20},{20... | collective-permute-start | bytes 7151624 | tf_op jit(solution)/shard_map/ppermute | solution.py:248
  582.6 15.3 %copy-start.27 = (bf16[1088,768]{1,0:T(8,128)(2,1)}, bf16[1088,768]{1,0:T(8,128)(2,1)S(1)}, u32[]{:S(2)}) copy-start(bf16[1088,768]{1,0:T(8,128)(2,1)S(1)} %reshape.399) | copy-start | bytes 5013508
  613.1 50.3 %all-to-all-start.7 = ((bf16[16,68,768]{2,1,0:T(8,128)(2,1)}), bf16[16,68,768]{2,1,0:T(8,128)(2,1)S(1)}, u32[]{:S(2)}, u32[]{:S(2)}) async-start(bf16[16,68,768]{2,1,0:T(8,128)(2,1)} %reshape.400), calls=%async_computation.7 | async-start | bytes 3538944 | tf_op jit(solution)/shard_map/all_to_all | solution.py:120
  621.8 14.4 %copy-start.81 = (f32[512]{0:T(512)S(1)}, f32[512]{0:T(512)}, u32[]{:S(2)}) copy-start(f32[512]{0:T(512)} %copy-done.80) | copy-start | bytes 6148
  621.9 14.4 %copy-start.88 = (f32[512]{0:T(512)S(1)}, f32[512]{0:T(512)}, u32[]{:S(2)}) copy-start(f32[512]{0:T(512)} %get-tuple-element.44) | copy-start | bytes 6148
  621.9 14.5 %copy-start.14 = (bf16[512,768]{1,0:T(8,128)(2,1)S(1)}, bf16[512,768]{1,0:T(8,128)(2,1)}, u32[]{:S(2)}) copy-start(bf16[512,768]{1,0:T(8,128)(2,1)} %copy-done.13) | copy-start | bytes 2359300
  621.9 14.5 %copy-start.62 = (s32[512,1]{0,1:T(1,128)S(1)}, s32[512,1]{0,1:T(1,128)}, u32[]{:S(2)}) copy-start(s32[512,1]{0,1:T(1,128)} %copy-done.61) | copy-start | bytes 6148
  621.9 14.5 %copy-start.64 = (s32[512,1]{0,1:T(1,128)S(1)}, s32[512,1]{0,1:T(1,128)}, u32[]{:S(2)}) copy-start(s32[512,1]{0,1:T(1,128)} %copy-done.63) | copy-start | bytes 6148
  621.9 165.5 %all-reduce.5.cloned.1.call-start = ((), (), s32[]{:S(2)}) async-start(), calls=%async_computation.12 | async-start | bytes 4767744 | tf_op jit(solution)/shard_map/psum | solution.py:249
  632.4 192.3 %collective-permute-start.8 = (bf16[768,3072]{1,0:T(8,128)(2,1)}, bf16[768,3072]{1,0:T(8,128)(2,1)}, u32[]{:S(2)}, u32[]{:S(2)}) collective-permute-start(bf16[768,3072]{1,0:T(8,128)(2,1)} %convolution_convert_fusion.2), channel_id=1, source_target_pairs={{0,16},{1,17},{2,18},{3,19},{4,20},{5,21},{6,22},{7,23},{8,24},{9,... | collective-permute-start | bytes 14155784 | tf_op jit(solution)/shard_map/ppermute | solution.py:314
  633.7 325.9 %collective-permute-start.10 = (bf16[3072,768]{1,0:T(8,128)(2,1)}, bf16[3072,768]{1,0:T(8,128)(2,1)}, u32[]{:S(2)}, u32[]{:S(2)}) collective-permute-start(bf16[3072,768]{1,0:T(8,128)(2,1)} %convolution_convert_fusion), channel_id=1, source_target_pairs={{0,16},{1,17},{2,18},{3,19},{4,20},{5,21},{6,22},{7,23},{8,24},{9,... | collective-permute-start | bytes 14155784 | tf_op jit(solution)/shard_map/ppermute | solution.py:315
  635.0 167.6 %collective-permute-start.1 = (bf16[512,768]{1,0:T(8,128)(2,1)}, bf16[512,768]{1,0:T(8,128)(2,1)}, u32[]{:S(2)}, u32[]{:S(2)}) collective-permute-start(bf16[512,768]{1,0:T(8,128)(2,1)} %get-tuple-element.45), channel_id=1, source_target_pairs={{0,16},{1,17},{2,18},{3,19},{4,20},{5,21},{6,22},{7,23},{8,24},{9,... | collective-permute-start | bytes 2359304 | tf_op jit(solution)/shard_map/ppermute | solution.py:316
  641.2 301.4 %all-reduce.7.cloned.1.call-start = ((), (), s32[]{:S(2)}) async-start(), calls=%async_computation.13 | async-start | bytes 4767744 | tf_op jit(solution)/shard_map/psum | solution.py:249
  652.1 294.6 %collective-permute-start.7 = (bf16[768,3072]{1,0:T(8,128)(2,1)}, bf16[768,3072]{1,0:T(8,128)(2,1)}, u32[]{:S(2)}, u32[]{:S(2)}) collective-permute-start(bf16[768,3072]{1,0:T(8,128)(2,1)} %convolution_convert_fusion.3), channel_id=1, source_target_pairs={{16,0},{17,1},{18,2},{19,3},{20,4},{21,5},{22,6},{23,7},{24,8},{25... | collective-permute-start | bytes 14155784 | tf_op jit(solution)/shard_map/ppermute | solution.py:320
  672.0 17.4 %slice-start = ((s8[12582912]{0:T(1024)(128)(4,1)}), s8[4194304]{0:T(1024)(128)(4,1)S(1)}, s32[]{:S(2)}) async-start(s8[12582912]{0:T(1024)(128)(4,1)} %bitcast.233), calls=%async_computation.14 | async-start | bytes 8388608
  672.0 17.4 %slice-start.1 = ((s8[12582912]{0:T(1024)(128)(4,1)}), s8[4194304]{0:T(1024)(128)(4,1)S(1)}, s32[]{:S(2)}) async-start(s8[12582912]{0:T(1024)(128)(4,1)} %bitcast.233), calls=%async_computation.15 | async-start | bytes 8388608
  720.2 69.5 %copy-start.28 = (bf16[1088,768]{1,0:T(8,128)(2,1)S(1)}, bf16[1088,768]{1,0:T(8,128)(2,1)}, u32[]{:S(2)}) copy-start(bf16[1088,768]{1,0:T(8,128)(2,1)} %copy-done.27) | copy-start | bytes 5013508
  789.2 17.5 %collective-permute-start.4 = (bf16[1552,768]{1,0:T(8,128)(2,1)S(1)}, bf16[1552,768]{1,0:T(8,128)(2,1)S(1)}, u32[]{:S(2)}, u32[]{:S(2)}) collective-permute-start(bf16[1552,768]{1,0:T(8,128)(2,1)S(1)} %constant_dynamic-slice_fusion), channel_id=1, source_target_pairs={{0,16},{16,0},{1,17},{17,1},{2,18},{18,2},{3,19},{19,3},{4,20},{20... | collective-permute-start | bytes 7151624 | tf_op jit(solution)/shard_map/ppermute | solution.py:248
  802.6 157.0 %collective-permute-start.9 = (bf16[3072,768]{1,0:T(8,128)(2,1)}, bf16[3072,768]{1,0:T(8,128)(2,1)}, u32[]{:S(2)}, u32[]{:S(2)}) collective-permute-start(bf16[3072,768]{1,0:T(8,128)(2,1)} %convolution_convert_fusion.1), channel_id=1, source_target_pairs={{16,0},{17,1},{18,2},{19,3},{20,4},{21,5},{22,6},{23,7},{24,8},{25... | collective-permute-start | bytes 14155784 | tf_op jit(solution)/shard_map/ppermute | solution.py:321
  806.7 7.3 collective-permute-start
  814.0 5.4 collective-permute-start.2
  820.1 150.4 %collective-permute-start.5 = (bf16[1552,768]{1,0:T(8,128)(2,1)S(1)}, bf16[1552,768]{1,0:T(8,128)(2,1)}, u32[]{:S(2)}, u32[]{:S(2)}) collective-permute-start(bf16[1552,768]{1,0:T(8,128)(2,1)S(1)} %copy-done.26), channel_id=1, source_target_pairs={{0,16},{1,17},{2,18},{3,19},{4,20},{5,21},{6,22},{7,23},{8,24},{9,... | collective-permute-start | bytes 7151624 | tf_op jit(solution)/shard_map/ppermute | solution.py:318
  942.6 29.9 %collective-permute-start.6 = (bf16[1552,768]{1,0:T(8,128)(2,1)}, bf16[1552,768]{1,0:T(8,128)(2,1)}, u32[]{:S(2)}, u32[]{:S(2)}) collective-permute-start(bf16[1552,768]{1,0:T(8,128)(2,1)} %all-reduce.7.cloned.1.call-done), channel_id=1, source_target_pairs={{16,0},{17,1},{18,2},{19,3},{20,4},{21,5},{22,6},{23,7},{24,8},{25... | collective-permute-start | bytes 7151624 | tf_op jit(solution)/shard_map/ppermute | solution.py:325
  (113 other events, 392.4 us)
Sparse Core Ops, SparseCore 0:
  9.6 20.3 all-gather.4
  31.5 12.1 all-gather.6
  45.2 23.0 all-gather.8
  69.7 23.0 all-gather.10
  641.3 146.0 all-reduce.4
  810.7 131.7 all-reduce.6
where the time goes:
time: 999 us; the launch traced here: 987 us
  waiting for transfers between devices  315 us (32%)
  matrix products  265 us (27%)
  blocking collectives  164 us (16%)
  local copies, waits for them, and re-layouts  87.3 us (9%)
  other arithmetic  77.3 us (8%)
  starting transfers between devices  61.8 us (6%)
  between operations  16.7 us (2%)
    dot_general x48, matrix products, dot(): lax.dot_general(a, b, (dims, ((), ())), precision=precision, preferred_el...  209 us
    psum x2, waiting for transfers between devices, reduce_shared(): return lax.psum((own.astype(F32) + other.astype(F32)).astype(BF), 'expert')  185 us
    all_to_all x3, blocking collectives, exchange(): lax.all_to_all(rows.reshape(experts, total // experts, width), 'expert',...  159 us
    all_to_all x5, waiting for transfers between devices, exchange(): lax.all_to_all(rows.reshape(experts, total // experts, width), 'expert',...  111 us
    all_to_all x5, starting transfers between devices, exchange(): lax.all_to_all(rows.reshape(experts, total // experts, width), 'expert',...  32.1 us
    reshape x8, local copies, waits for them, and re-layouts, exchange(): rows.reshape(experts, total // experts, width)  27.2 us
    unnamed x278, local copies, waits for them, and re-layouts  23.3 us
    reshape x8, local copies, waits for them, and re-layouts, exchange(): return moved.reshape(total, width)  23.1 us
  transfers between devices with their start and end apart: 22, of which 8 were waited for; matrix products, arithmetic and copies ran while one was open for 23% of the time, Pallas kernels for 0%

commit v1 on v0

--- a/solution.py
+++ b/solution.py
@@ -246,7 +246,9 @@
     own = lax.dynamic_slice_in_dim(shared, section * half, half, 0)
     other = lax.dynamic_slice_in_dim(shared, (1 - section) * half, half, 0)
     other = lax.ppermute(other, "section", SWAP)
-    return lax.psum((own.astype(F32) + other.astype(F32)).astype(BF), "expert")
+    return jnp.sum(
+        lax.all_gather((own.astype(F32) + other.astype(F32)).astype(BF), "expert"), axis=0
+    )
 
 
 def both(own, other, is_first):

time: 999 us -> 1510 us (1.51)
  waiting for transfers between devices: 315 us -> 724 us
  blocking collectives: 164 us -> 256 us
  other arithmetic: 77.3 us -> 102 us
    all_gather x0 -> x2, waiting for transfers between devices: none -> 525 us  [reduce_shared(): lax.all_gather((own.astype(F32) + other.astype(F32)).astype(BF), 'expert')]
    psum x2 -> x0, waiting for transfers between devices: 185 us -> none  [reduce_shared(): return lax.psum((own.astype(F32) + other.astype(F32)).astype(BF), 'expert')]
    all_to_all x3 -> x4, blocking collectives: 159 us -> 251 us  [exchange(): lax.all_to_all(rows.reshape(experts, total // experts, width), 'expert',...]
    all_to_all x5 -> x4, waiting for transfers between devices: 111 us -> 165 us  [exchange(): lax.all_to_all(rows.reshape(experts, total // experts, width), 'expert',...]
    reduce_sum x0 -> x2, other arithmetic: none -> 29.7 us  [reduce_shared(): jnp.sum(lax.all_gather((own.astype(F32) + other.astype(F32)).astype(BF),...]
    all_to_all x5 -> x4, starting transfers between devices: 32.1 us -> 18.1 us  [exchange(): lax.all_to_all(rows.reshape(experts, total // experts, width), 'expert',...]
  transfers between devices with their start and end apart: 22 -> 21, of which waited for: 8 -> 11; matrix products, arithmetic and copies ran while one was open for 23% -> 15% of each run, Pallas kernels for 0% -> 0%
where the time goes in v1:
time: 1510 us; the launch traced here: 1500 us
  waiting for transfers between devices  724 us (48%)
  matrix products  267 us (18%)
  blocking collectives  256 us (17%)
  other arithmetic  102 us (7%)
  local copies, waits for them, and re-layouts  83 us (5%)
  starting transfers between devices  47.8 us (3%)
  between operations  16.7 us (1%)
    all_gather x2, waiting for transfers between devices, reduce_shared(): lax.all_gather((own.astype(F32) + other.astype(F32)).astype(BF), 'expert')  525 us
    all_to_all x4, blocking collectives, exchange(): lax.all_to_all(rows.reshape(experts, total // experts, width), 'expert',...  251 us
    dot_general x48, matrix products, dot(): lax.dot_general(a, b, (dims, ((), ())), precision=precision, preferred_el...  210 us
    all_to_all x4, waiting for transfers between devices, exchange(): lax.all_to_all(rows.reshape(experts, total // experts, width), 'expert',...  165 us
  transfers between devices with their start and end apart: 21, of which 11 were waited for; matrix products, arithmetic and copies ran while one was open for 15% of the time, Pallas kernels for 0%

profile of v1, /device:TPU:1, one launch (start us, length us, event | category | flops | bytes accessed | tf_op | source)
XLA Modules:
  0.0 1496.3 jit_solution(1025594737205559084)
XLA Ops:
  14.0 15.9 %all-gather.9.cloned.1.call-done = bf16[2,768,2304]{2,1,0:T(8,128)(2,1)} async-done(((bf16[1,768,2304]{2,1,0:T(8,128)(2,1)}), bf16[2,768,2304]{2,1,0:T(8,128)(2,1)}) %all-gather.9.cloned.1.call-update) | async-done | bytes 7077904 | tf_op jit(solution)/shard_map/all_gather | solution.py:281
  55.3 58.5 %all_to_all.40 = bf16[16,68,768]{2,1,0:T(8,128)(2,1)} all-to-all(bf16[16,68,768]{2,1,0:T(8,128)(2,1)} %reshape.378), channel_id=1, replica_groups=mesh['section'=2,'expert'=16] {'expert'}, dimensions={0} | all-to-all | bytes 3342336 | tf_op jit(solution)/shard_map/all_to_all | solution.py:120
  117.2 10.9 fusion.19
  128.1 13.0 fusion.26
  144.5 4.6 all-to-all-start.1
  154.8 30.5 %all-to-all-done.1 = bf16[16,68,768]{2,1,0:T(8,128)(2,1)} async-done(((bf16[16,68,768]{2,1,0:T(8,128)(2,1)}), bf16[16,68,768]{2,1,0:T(8,128)(2,1)}, u32[]{:S(2)}, u32[]{:S(2)}) %all-to-all-start.1) | async-done | bytes 1671200 | tf_op jit(solution)/shard_map/all_to_all | solution.py:120
  192.2 4.4 fusion.33
  215.6 50.3 %all_to_all.41 = bf16[16,68,768]{2,1,0:T(8,128)(2,1)} all-to-all(bf16[16,68,768]{2,1,0:T(8,128)(2,1)} %reshape.386), channel_id=1, replica_groups=mesh['section'=2,'expert'=16] {'expert'}, dimensions={0} | all-to-all | bytes 3342336 | tf_op jit(solution)/shard_map/all_to_all | solution.py:120
  269.3 7.7 fusion.22
  277.0 4.8 copy-done.127
  281.8 11.3 fusion.24
  296.5 4.7 all-to-all-start.3
  301.6 35.7 %all-to-all-done.3 = bf16[16,68,768]{2,1,0:T(8,128)(2,1)} async-done(((bf16[16,68,768]{2,1,0:T(8,128)(2,1)}), bf16[16,68,768]{2,1,0:T(8,128)(2,1)}, u32[]{:S(2)}, u32[]{:S(2)}) %all-to-all-start.3) | async-done | bytes 1671200 | tf_op jit(solution)/shard_map/all_to_all | solution.py:120
  353.1 50.5 %all_to_all.42 = bf16[16,68,768]{2,1,0:T(8,128)(2,1)} all-to-all(bf16[16,68,768]{2,1,0:T(8,128)(2,1)} %reshape.390), channel_id=1, replica_groups=mesh['section'=2,'expert'=16] {'expert'}, dimensions={0} | all-to-all | bytes 3342336 | tf_op jit(solution)/shard_map/all_to_all | solution.py:120
  407.0 15.1 %fusion = bf16[1088,3072]{1,0:T(8,128)(2,1)S(1)} fusion(bf16[1088,768]{1,0:T(8,128)(2,1)} %reshape.391, f32[1088,3072]{1,0:T(8,128)} %copy-done.127, bf16[2,1,3072,768]{3,2,1,0:T(8,128)(2,1)} %all-gather.15.cloned.1.call-done), kind=kOutput, calls=%fused_computation.22 | convolution fusion | flops 5200674816 | bytes 26443776 | tf_op jit(solution)/shard_map/dot_general | solution.py:16
  424.9 8.9 fusion.25
  437.2 4.6 all-to-all-start.5
  442.3 35.6 %all-to-all-done.5 = bf16[16,68,768]{2,1,0:T(8,128)(2,1)} async-done(((bf16[16,68,768]{2,1,0:T(8,128)(2,1)}), bf16[16,68,768]{2,1,0:T(8,128)(2,1)}, u32[]{:S(2)}, u32[]{:S(2)}) %all-to-all-start.5) | async-done | bytes 1671200 | tf_op jit(solution)/shard_map/all_to_all | solution.py:120
  490.6 8.0 bitcast_reduce_fusion.2
  498.6 9.6 multiply_reduce_fusion.1
  508.2 7.2 multiply_convert_fusion.3
  521.8 5.4 fusion.84
  539.8 4.5 collective-permute-done.3
  544.3 4.4 add_convert_fusion.3
  558.6 91.9 %all_to_all.43 = bf16[16,68,768]{2,1,0:T(8,128)(2,1)} all-to-all(bf16[16,68,768]{2,1,0:T(8,128)(2,1)S(1)} %reshape.398), channel_id=1, replica_groups=mesh['section'=2,'expert'=16] {'expert'}, dimensions={0} | all-to-all | bytes 3342336 | tf_op jit(solution)/shard_map/all_to_all | solution.py:120
  652.9 15.3 %fusion.1 = bf16[1088,3072]{1,0:T(8,128)(2,1)S(1)} fusion(bf16[1088,768]{1,0:T(8,128)(2,1)S(1)} %reshape.399, f32[1088,3072]{1,0:T(8,128)} %fusion.19, bf16[2,1,3072,768]{3,2,1,0:T(8,128)(2,1)} %all-gather.15.cloned.1.call-done), kind=kOutput, calls=%fused_computation.23 | convolution fusion | flops 5200674816 | bytes 26443776 | tf_op jit(solution)/shard_map/dot_general | solution.py:16
  670.9 9.0 fusion.27
  683.3 4.2 all-to-all-start.7
  688.1 62.8 %all-to-all-done.7 = bf16[16,68,768]{2,1,0:T(8,128)(2,1)S(1)} async-done(((bf16[16,68,768]{2,1,0:T(8,128)(2,1)}), bf16[16,68,768]{2,1,0:T(8,128)(2,1)S(1)}, u32[]{:S(2)}, u32[]{:S(2)}) %all-to-all-start.7) | async-done | bytes 1671200 | tf_op jit(solution)/shard_map/all_to_all | solution.py:120
  760.6 8.9 bitcast_reduce_fusion
  769.6 7.5 multiply_reduce_fusion
  777.1 7.2 multiply_convert_fusion.2
  787.4 4.9 multiply_convert_fusion.4
  792.4 5.7 fusion.74
  808.1 210.4 %all-gather.17.cloned.1.call-done = bf16[24832,768]{1,0:T(8,128)(2,1)} async-done(((bf16[1552,768]{1,0:T(8,128)(2,1)}), bf16[24832,768]{1,0:T(8,128)(2,1)}) %all-gather.17.cloned.1.call-update) | async-done | bytes 38141968 | tf_op jit(solution)/shard_map/all_gather | solution.py:250
  1018.5 14.9 reduce_sum.340
  1036.4 4.2 collective-permute-done.4
  1044.4 10.8 convolution_convert_fusion.2
  1056.7 12.7 convolution_convert_fusion
  1072.2 7.9 convolution_convert_fusion.3
  1080.1 9.7 collective-permute-start.7
  1089.8 12.9 convolution_convert_fusion.1
  1106.8 5.9 collective-permute-done
  1122.0 314.2 %all-gather.19.cloned.1.call-done = bf16[24832,768]{1,0:T(8,128)(2,1)} async-done(((bf16[1552,768]{1,0:T(8,128)(2,1)}), bf16[24832,768]{1,0:T(8,128)(2,1)}) %all-gather.19.cloned.1.call-update) | async-done | bytes 38141968 | tf_op jit(solution)/shard_map/all_gather | solution.py:250
  1436.2 14.8 reduce_sum.341
  1451.0 4.7 collective-permute-start.6
  1455.7 12.9 fusion.14
  1468.6 10.9 fusion.15
  (428 shorter events, 209.1 us)
Async XLA Ops:
  7.2 22.8 %all-gather.9.cloned.1.call-start = ((), (), s32[]{:S(2)}) async-start(), calls=%async_computation.8 | async-start | bytes 10616832 | tf_op jit(solution)/shard_map/all_gather | solution.py:281
  7.9 38.5 %all-gather.11.cloned.1.call-start = ((), (), s32[]{:S(2)}) async-start(), calls=%async_computation.9 | async-start | bytes 3538944 | tf_op jit(solution)/shard_map/all_gather | solution.py:281
  8.7 108.6 %all-gather.13.cloned.1.call-start = ((), (), s32[]{:S(2)}) async-start(), calls=%async_computation.10 | async-start | bytes 14155776 | tf_op jit(solution)/shard_map/all_gather | solution.py:281
  9.5 118.7 %all-gather.15.cloned.1.call-start = ((), (), s32[]{:S(2)}) async-start(), calls=%async_computation.11 | async-start | bytes 14155776 | tf_op jit(solution)/shard_map/all_gather | solution.py:281
  11.1 18.9 %copy-start.94 = (f32[512]{0:T(512)}, f32[512]{0:T(512)S(1)}, u32[]{:S(2)}) copy-start(f32[512]{0:T(512)S(1)} %add_rsqrt_fusion.3) | copy-start | bytes 6148
  11.1 141.5 %copy-start.67 = (s32[512,1]{0,1:T(1,128)}, s32[512,1]{0,1:T(1,128)S(1)}, u32[]{:S(2)}) copy-start(s32[512,1]{0,1:T(1,128)S(1)} %get-tuple-element.69) | copy-start | bytes 6148
  11.1 142.1 %copy-start.71 = (s32[512,1]{0,1:T(1,128)}, s32[512,1]{0,1:T(1,128)S(1)}, u32[]{:S(2)}) copy-start(s32[512,1]{0,1:T(1,128)S(1)} %get-tuple-element.70) | copy-start | bytes 6148
  11.1 142.7 %copy-start.63 = (s32[512,1]{0,1:T(1,128)}, s32[512,1]{0,1:T(1,128)S(1)}, u32[]{:S(2)}) copy-start(s32[512,1]{0,1:T(1,128)S(1)} %get-tuple-element.105) | copy-start | bytes 6148
  11.1 142.7 %copy-start.65 = (s32[512,1]{0,1:T(1,128)}, s32[512,1]{0,1:T(1,128)S(1)}, u32[]{:S(2)}) copy-start(s32[512,1]{0,1:T(1,128)S(1)} %get-tuple-element.106) | copy-start | bytes 6148
  11.4 38.0 %copy-start.108 = (s32[512]{0:T(512)}, s32[512]{0:T(512)S(1)}, u32[]{:S(2)}) copy-start(s32[512]{0:T(512)S(1)} %convert_add_fusion.8) | copy-start | bytes 6148
  11.4 37.9 %copy-start.110 = (s32[512]{0:T(512)}, s32[512]{0:T(512)S(1)}, u32[]{:S(2)}) copy-start(s32[512]{0:T(512)S(1)} %convert_add_fusion.7) | copy-start | bytes 6148
  14.0 15.9 %copy-start.84 = (f32[768]{0:T(1024)}, f32[768]{0:T(1024)S(1)}, u32[]{:S(2)}) copy-start(f32[768]{0:T(1024)S(1)} %get-tuple-element.33) | copy-start | bytes 9220
  14.0 35.1 %copy-start.59 = (f32[768]{0:T(1024)}, f32[768]{0:T(1024)S(1)}, u32[]{:S(2)}) copy-start(f32[768]{0:T(1024)S(1)} %get-tuple-element.29) | copy-start | bytes 9220
  49.1 140.6 %copy-start.3 = (f32[512,768]{1,0:T(8,128)}, f32[512,768]{1,0:T(8,128)S(1)}, u32[]{:S(2)}) copy-start(f32[512,768]{1,0:T(8,128)S(1)} %get-tuple-element.81) | copy-start | bytes 4718596
  49.4 104.4 %copy-start.14 = (bf16[512,768]{1,0:T(8,128)(2,1)}, bf16[512,768]{1,0:T(8,128)(2,1)S(1)}, u32[]{:S(2)}) copy-start(bf16[512,768]{1,0:T(8,128)(2,1)S(1)} %multiply_convert_fusion.9) | copy-start | bytes 2359300
  144.5 40.7 %all-to-all-start.1 = ((bf16[16,68,768]{2,1,0:T(8,128)(2,1)}), bf16[16,68,768]{2,1,0:T(8,128)(2,1)}, u32[]{:S(2)}, u32[]{:S(2)}) async-start(bf16[16,68,768]{2,1,0:T(8,128)(2,1)} %reshape.380), calls=%async_computation.1 | async-start | bytes 3538944 | tf_op jit(solution)/shard_map/all_to_all | solution.py:120
  296.5 40.8 %all-to-all-start.3 = ((bf16[16,68,768]{2,1,0:T(8,128)(2,1)}), bf16[16,68,768]{2,1,0:T(8,128)(2,1)}, u32[]{:S(2)}, u32[]{:S(2)}) async-start(bf16[16,68,768]{2,1,0:T(8,128)(2,1)} %reshape.388), calls=%async_computation.3 | async-start | bytes 3538944 | tf_op jit(solution)/shard_map/all_to_all | solution.py:120
  346.0 95.9 %copy-start.80 = (f32[512]{0:T(512)}, f32[512]{0:T(512)S(1)}, u32[]{:S(2)}) copy-start(f32[512]{0:T(512)S(1)} %get-tuple-element.73) | copy-start | bytes 6148
  437.2 40.7 %all-to-all-start.5 = ((bf16[16,68,768]{2,1,0:T(8,128)(2,1)}), bf16[16,68,768]{2,1,0:T(8,128)(2,1)}, u32[]{:S(2)}, u32[]{:S(2)}) async-start(bf16[16,68,768]{2,1,0:T(8,128)(2,1)} %reshape.392), calls=%async_computation.5 | async-start | bytes 3538944 | tf_op jit(solution)/shard_map/all_to_all | solution.py:120
  441.8 576.7 %all-gather.17.cloned.1.call-start = ((), (), s32[]{:S(2)}) async-start(), calls=%async_computation.12 | async-start | bytes 40525824 | tf_op jit(solution)/shard_map/all_gather | solution.py:250
  490.5 17.6 %slice-start = ((s8[12582912]{0:T(1024)(128)(4,1)}), s8[4194304]{0:T(1024)(128)(4,1)S(1)}, s32[]{:S(2)}) async-start(s8[12582912]{0:T(1024)(128)(4,1)} %bitcast.235), calls=%async_computation.14 | async-start | bytes 8388608
  490.6 17.6 %slice-start.1 = ((s8[12582912]{0:T(1024)(128)(4,1)}), s8[4194304]{0:T(1024)(128)(4,1)S(1)}, s32[]{:S(2)}) async-start(s8[12582912]{0:T(1024)(128)(4,1)} %bitcast.235), calls=%async_computation.15 | async-start | bytes 8388608
  498.6 9.6 slice-start.2
  537.2 7.1 collective-permute-start.3
  652.9 15.3 %copy-start.32 = (bf16[1088,768]{1,0:T(8,128)(2,1)}, bf16[1088,768]{1,0:T(8,128)(2,1)S(1)}, u32[]{:S(2)}) copy-start(bf16[1088,768]{1,0:T(8,128)(2,1)S(1)} %reshape.399) | copy-start | bytes 5013508
  683.3 67.6 %all-to-all-start.7 = ((bf16[16,68,768]{2,1,0:T(8,128)(2,1)}), bf16[16,68,768]{2,1,0:T(8,128)(2,1)S(1)}, u32[]{:S(2)}, u32[]{:S(2)}) async-start(bf16[16,68,768]{2,1,0:T(8,128)(2,1)} %reshape.400), calls=%async_computation.7 | async-start | bytes 3538944 | tf_op jit(solution)/shard_map/all_to_all | solution.py:120
  687.5 748.7 %all-gather.19.cloned.1.call-start = ((), (), s32[]{:S(2)}) async-start(), calls=%async_computation.13 | async-start | bytes 40525824 | tf_op jit(solution)/shard_map/all_gather | solution.py:250
  760.6 9.0 copy-start.24
  1035.2 5.3 collective-permute-start.4
  1044.4 12.3 copy-start.31
  1044.4 27.7 %slice-start.3 = ((s8[6684672]{0:T(1024)(128)(4,1)}), s8[4194304]{0:T(1024)(128)(4,1)S(1)}, s32[]{:S(2)}) async-start(s8[6684672]{0:T(1024)(128)(4,1)} %bitcast.296), calls=%async_computation.17 | async-start | bytes 8388608
  1055.2 17.0 %copy-start.30 = (bf16[1088,768]{1,0:T(8,128)(2,1)S(1)}, bf16[1088,768]{1,0:T(8,128)(2,1)}, u32[]{:S(2)}) copy-start(bf16[1088,768]{1,0:T(8,128)(2,1)} %reshape.379) | copy-start | bytes 5013508
  1055.2 17.0 %slice-start.4 = ((s8[6684672]{0:T(1024)(128)(4,1)}), s8[2490368]{0:T(1024)(128)(4,1)S(1)}, s32[]{:S(2)}) async-start(s8[6684672]{0:T(1024)(128)(4,1)} %bitcast.296), calls=%async_computation.18 | async-start | bytes 4980736
  1055.2 395.8 %collective-permute-start.8 = (bf16[768,3072]{1,0:T(8,128)(2,1)}, bf16[768,3072]{1,0:T(8,128)(2,1)}, u32[]{:S(2)}, u32[]{:S(2)}) collective-permute-start(bf16[768,3072]{1,0:T(8,128)(2,1)} %convolution_convert_fusion.2), channel_id=1, source_target_pairs={{0,16},{1,17},{2,18},{3,19},{4,20},{5,21},{6,22},{7,23},{8,24},{9,... | collective-permute-start | bytes 14155784 | tf_op jit(solution)/shard_map/ppermute | solution.py:316
  1069.4 20.4 %copy-start.33 = (bf16[1088,768]{1,0:T(8,128)(2,1)S(1)}, bf16[1088,768]{1,0:T(8,128)(2,1)}, u32[]{:S(2)}) copy-start(bf16[1088,768]{1,0:T(8,128)(2,1)} %copy-done.32) | copy-start | bytes 5013508
  1069.4 399.2 %collective-permute-start.10 = (bf16[3072,768]{1,0:T(8,128)(2,1)}, bf16[3072,768]{1,0:T(8,128)(2,1)}, u32[]{:S(2)}, u32[]{:S(2)}) collective-permute-start(bf16[3072,768]{1,0:T(8,128)(2,1)} %convolution_convert_fusion), channel_id=1, source_target_pairs={{0,16},{1,17},{2,18},{3,19},{4,20},{5,21},{6,22},{7,23},{8,24},{9,... | collective-permute-start | bytes 14155784 | tf_op jit(solution)/shard_map/ppermute | solution.py:317
  1070.8 35.3 %collective-permute-start.1 = (bf16[512,768]{1,0:T(8,128)(2,1)S(1)}, bf16[512,768]{1,0:T(8,128)(2,1)S(1)}, u32[]{:S(2)}, u32[]{:S(2)}) collective-permute-start(bf16[512,768]{1,0:T(8,128)(2,1)S(1)} %copy-done.22), channel_id=1, source_target_pairs={{0,16},{1,17},{2,18},{3,19},{4,20},{5,21},{6,22},{7,23},{8,24},{9,... | collective-permute-start | bytes 2359304 | tf_op jit(solution)/shard_map/ppermute | solution.py:318
  1080.1 26.1 %copy-start.42 = (bf16[512,768]{1,0:T(8,128)(2,1)S(1)}, bf16[512,768]{1,0:T(8,128)(2,1)}, u32[]{:S(2)}) copy-start(bf16[512,768]{1,0:T(8,128)(2,1)} %get-tuple-element.65) | copy-start | bytes 2359300
  1080.1 26.1 %copy-start.35 = (f32[512,768]{1,0:T(8,128)S(1)}, f32[512,768]{1,0:T(8,128)}, u32[]{:S(2)}) copy-start(f32[512,768]{1,0:T(8,128)} %get-tuple-element.96) | copy-start | bytes 4718596
  1080.1 26.1 %copy-start.39 = (bf16[2,512,768]{2,1,0:T(8,128)(2,1)S(1)}, bf16[2,512,768]{2,1,0:T(8,128)(2,1)}, u32[]{:S(2)}) copy-start(bf16[2,512,768]{2,1,0:T(8,128)(2,1)} %param.13) | copy-start | bytes 4718596
  1080.1 375.6 %collective-permute-start.7 = (bf16[768,3072]{1,0:T(8,128)(2,1)}, bf16[768,3072]{1,0:T(8,128)(2,1)}, u32[]{:S(2)}, u32[]{:S(2)}) collective-permute-start(bf16[768,3072]{1,0:T(8,128)(2,1)} %convolution_convert_fusion.3), channel_id=1, source_target_pairs={{16,0},{17,1},{18,2},{19,3},{20,4},{21,5},{22,6},{23,7},{24,8},{25... | collective-permute-start | bytes 14155784 | tf_op jit(solution)/shard_map/ppermute | solution.py:322
  1102.7 365.9 %collective-permute-start.9 = (bf16[3072,768]{1,0:T(8,128)(2,1)}, bf16[3072,768]{1,0:T(8,128)(2,1)}, u32[]{:S(2)}, u32[]{:S(2)}) collective-permute-start(bf16[3072,768]{1,0:T(8,128)(2,1)} %convolution_convert_fusion.1), channel_id=1, source_target_pairs={{16,0},{17,1},{18,2},{19,3},{20,4},{21,5},{22,6},{23,7},{24,8},{25... | collective-permute-start | bytes 14155784 | tf_op jit(solution)/shard_map/ppermute | solution.py:323
  1106.1 6.5 collective-permute-start
  1106.2 8.8 copy-start.20
  1106.2 8.8 copy-start.27
  1112.7 5.3 collective-permute-start.2
  1120.7 358.9 %collective-permute-start.5 = (bf16[1552,768]{1,0:T(8,128)(2,1)S(1)}, bf16[1552,768]{1,0:T(8,128)(2,1)}, u32[]{:S(2)}, u32[]{:S(2)}) collective-permute-start(bf16[1552,768]{1,0:T(8,128)(2,1)S(1)} %copy-done.9), channel_id=1, source_target_pairs={{0,16},{1,17},{2,18},{3,19},{4,20},{5,21},{6,22},{7,23},{8,24},{9,... | collective-permute-start | bytes 7151624 | tf_op jit(solution)/shard_map/ppermute | solution.py:320
  1451.0 30.5 %collective-permute-start.6 = (bf16[1552,768]{1,0:T(8,128)(2,1)}, bf16[1552,768]{1,0:T(8,128)(2,1)}, u32[]{:S(2)}, u32[]{:S(2)}) collective-permute-start(bf16[1552,768]{1,0:T(8,128)(2,1)} %reduce_sum.341), channel_id=1, source_target_pairs={{16,0},{17,1},{18,2},{19,3},{20,4},{21,5},{22,6},{23,7},{24,8},{25... | collective-permute-start | bytes 7151624 | tf_op jit(solution)/shard_map/ppermute | solution.py:327
  (106 other events, 321.3 us)
Sparse Core Ops, SparseCore 0:
  9.6 20.3 all-gather.8
  31.5 12.1 all-gather.10
  45.2 23.0 all-gather.12
  69.7 23.0 all-gather.14
  548.9 469.5 all-gather.16
  1044.5 391.6 all-gather.18
